TPU v7x, 512 devices: a whole 4x8x8 slice. The times are simulated.
512 devices in a mesh: ex: 8 (over z), tp: 16 (over y_lo, x, core), blk: 4 (over y_hi).
Axes of the slice: x: 4, y: 8 (y_hi: 4, y_lo: 2; y = y_hi * 2 + y_lo), z: 8, core: 2. Of those that a mesh axis runs over, the one named last changes fastest.
Arguments:
- gradients: bfloat16 [2048, 32768], P('ex', 'tp'), may hold values from -6 to 6
- selection: int32 [1024], P('ex'), may hold values from 0 to 255, as said below
- seed_value: int32 [1], replicated, may hold values from 0 to 999999999
- ridge_value: float32 [1], replicated, may hold values from 0.3 to 3
Outputs:
- panel_out: float32 [8192, 512], P(('ex', 'blk'))
- trailing: float32 [8192, 8192], P(('ex', 'blk'), 'tp')
Inputs may be any that keep to these rules, and one draw needn't show every extreme that they name: `selection`: within each aligned block of 128 entries the values are distinct, and 0 and 255 occur in every block.
All inputs are finite; a program needn't handle non-finite values.
Results may differ from a plain program's by a relative error of at most 0.0046.
Values may be sent and summed in bfloat16 or wider, within the bound.
A program may use at most 64 MiB of HBM per device.

v0:
```python
import math

import jax
import jax.numpy as jnp
from jax import lax
from jax.sharding import PartitionSpec as P

PANEL = 512
HALF = 256


def from_root(value, axis, source):
    kept = jnp.where(lax.axis_index(axis) == source, value, 0).astype(value.dtype)
    return lax.psum(kept, axis)


def scramble(hashed, amount):
    return hashed ^ lax.shift_right_logical(hashed, jnp.full_like(hashed, amount))


def sign_block(seed_word, coordinates, features):
    hashed = (
        coordinates[:, None] * jnp.int32(-1640531535)
        + features[None, :] * jnp.int32(668265263)
        + seed_word
    )
    hashed = scramble(hashed, 16) * jnp.int32(-2048144789)
    hashed = scramble(hashed, 13) * jnp.int32(-1028477387)
    hashed = scramble(hashed, 16)
    bit_value = lax.shift_right_logical(hashed, jnp.full_like(hashed, 7)) & jnp.int32(1)
    return jnp.int32(1) - jnp.int32(2) * bit_value


def contract_rows(left_part, right_part):
    return lax.dot_general(
        left_part, right_part, (((0,), (0,)), ((), ())), preferred_element_type=jnp.float32
    )


def shards(gradients, selection, seed_value, ridge_value):
    ex_count = lax.axis_size("ex")
    tp_count = lax.axis_size("tp")
    blk_count = lax.axis_size("blk")
    tp_index = lax.axis_index("tp")
    group_index = lax.axis_index("ex") * blk_count + lax.axis_index("blk")
    example_rows_dev = selection.shape[0]
    coord_dev = gradients.shape[1]
    chosen = gradients[selection]
    feature_ids = (
        (jnp.arange(ex_count, dtype=jnp.int32)[:, None] * blk_count + lax.axis_index("blk")) * HALF
        + jnp.arange(HALF, dtype=jnp.int32)[None, :]
    ).reshape(-1)
    stride = min(512, coord_dev)
    projected = jnp.zeros((example_rows_dev, ex_count * HALF), jnp.float32)
    for segment in range(coord_dev // stride):
        coordinates = tp_index * coord_dev + segment * stride + jnp.arange(stride, dtype=jnp.int32)
        sign_values = sign_block(seed_value[0], coordinates, feature_ids).astype(jnp.bfloat16)
        projected = projected + jnp.dot(
            chosen[:, segment * stride : (segment + 1) * stride],
            sign_values,
            preferred_element_type=jnp.float32,
        )
    summed = lax.psum(projected, "tp")
    scaling = 1.0 / math.sqrt(coord_dev * tp_count)
    phi_columns = (summed * scaling).astype(jnp.bfloat16)
    row_parts = []
    gathered = lax.all_gather(phi_columns, "blk", axis=1, tiled=True)
    gathered = gathered.reshape(example_rows_dev, blk_count * ex_count, HALF)
    for which in range(2):
        owner_group = 2 * tp_index + which
        slot_index = owner_group % blk_count * ex_count + owner_group // blk_count
        row_parts.append(lax.dynamic_index_in_dim(gathered, slot_index, 1, keepdims=False))
    phi_rows = jnp.concatenate(row_parts, axis=1)
    examples = float(example_rows_dev * ex_count)
    summed_tile = lax.psum_scatter(
        contract_rows(phi_columns, phi_rows), "ex", scatter_dimension=0, tiled=True
    )
    row_features = group_index * HALF + jnp.arange(HALF, dtype=jnp.int32)
    column_features = tp_index * PANEL + jnp.arange(PANEL, dtype=jnp.int32)
    diag_mask = (row_features[:, None] == column_features[None, :]).astype(jnp.float32)
    own_tile = summed_tile / examples + ridge_value[0] * diag_mask
    top_pieces = [from_root(own_tile, ("ex", "blk"), which) for which in range(2)]
    top_block = jnp.concatenate(top_pieces, axis=0)
    diag_block, first_tile = (from_root(top_block, "tp", 0), from_root(own_tile, "tp", 0))
    factor = jnp.linalg.cholesky(diag_block)
    right_part = jax.scipy.linalg.solve_triangular(factor, top_block, lower=True)
    panel_out = jax.scipy.linalg.solve_triangular(factor, first_tile.T, lower=True).T
    trailing = own_tile - jnp.dot(panel_out, right_part, precision=lax.Precision.HIGHEST)
    return (panel_out, trailing)


def solution(mesh):
    in_specs = (P("ex", "tp"), P("ex"), P(), P())
    out_specs = (P(("ex", "blk"), None), P(("ex", "blk"), "tp"))
    return jax.shard_map(shards, mesh=mesh, in_specs=in_specs, out_specs=out_specs, check_vma=False)
```

profile of v0, /device:TPU:1, one launch (start us, length us, event | category | flops | bytes accessed | tf_op | source)
XLA Modules:
  0.0 905.8 jit_solution(9812928467145269872)
XLA Ops:
  8.1 0.7 compare_select_fusion
  8.8 0.9 gather_fusion
  9.7 2.4 fusion.58
  12.1 2.4 convolution_add_fusion.2
  14.6 2.4 convolution_add_fusion.1
  17.0 3.5 convolution_add_fusion
  20.6 135.6 %all-reduce.7.cloned.1.call-done = f32[128,2048]{1,0:T(8,128)} async-done(((f32[128,2048]{1,0:T(8,128)}), f32[128,2048]{1,0:T(8,128)}) %all-reduce.7.cloned.1.call-update) | async-done | bytes 1048592 | tf_op jit(solution)/shard_map/psum | solution.py:63
  156.2 2.1 multiply_convert_fusion
  158.4 51.3 %all-gather.2.cloned.1.call-done = bf16[128,8192]{1,0:T(8,128)(2,1)} async-done(((bf16[128,2048]{1,0:T(8,128)(2,1)}), bf16[128,8192]{1,0:T(8,128)(2,1)}) %all-gather.2.cloned.1.call-update) | async-done | bytes 2097168 | tf_op jit(solution)/shard_map/all_gather | solution.py:67
  209.7 2.2 copy.42
  212.2 2.7 fusion.101
  215.7 61.2 %reduce-scatter.2.cloned.1.call-done = f32[256,512]{0,1:T(8,128)} async-done(((f32[2048,512]{0,1:T(8,128)}), f32[256,512]{0,1:T(8,128)}) %reduce-scatter.2.cloned.1.call-update) | async-done | bytes 524304 | tf_op jit(solution)/shard_map/reduce_scatter | solution.py:75
  276.9 2.4 broadcast_select_fusion.1
  279.5 298.8 %all-reduce.9.cloned.1.call-done = (f32[256,512]{0,1:T(8,128)}, f32[256,512]{0,1:T(8,128)}) async-done(((f32[256,512]{0,1:T(8,128)}, f32[256,512]{0,1:T(8,128)}), (f32[256,512]{0,1:T(8,128)}, f32[256,512]{0,1:T(8,128)})) %all-reduce.9.cloned.1.call-update) | async-done | bytes 1048592 | tf_op jit(solution)/shard_map/psum | solution.py:14
  578.3 2.3 maximum_select_fusion
  581.2 149.0 %all-reduce.11.cloned.1.call-done = (f32[512,256]{1,0:T(8,128)}, f32[512,512]{0,1:T(8,128)}) async-done(((f32[512,256]{1,0:T(8,128)}, f32[512,512]{0,1:T(8,128)}), (f32[512,256]{1,0:T(8,128)}, f32[512,512]{0,1:T(8,128)})) %all-reduce.11.cloned.1.call-update) | async-done | bytes 1572880 | tf_op jit(solution)/shard_map/psum | solution.py:14
  730.2 1.6 copy.22
  731.8 1.4 fusion.67
  733.3 11.7 %cholesky.105 = f32[128,128]{1,0:T(8,128)S(1)} custom-call(f32[128,128]{1,0:T(8,128)S(1)} %cholesky.266), custom_call_target="Cholesky" | custom-call | tf_op jit(solution)/shard_map/jit(cholesky)/cholesky | solution.py:85
  745.0 0.7 copy.23
  745.7 9.8 %custom-call.34 = f32[1,128,128]{1,2,0:T(8,128)S(1)} custom-call(f32[1,128,128]{2,1,0:T(8,128)S(1)} %get-tuple-element.46), custom_call_target="InvertDiagBlocksLowerTriangular" | custom-call | tf_op jit(solution)/shard_map/jit(cholesky)/cholesky | solution.py:85
  756.4 11.7 %cholesky.218 = f32[128,128]{1,0:T(8,128)S(1)} custom-call(f32[128,128]{1,0:T(8,128)S(1)} %cholesky.270), custom_call_target="Cholesky" | custom-call | tf_op jit(solution)/shard_map/jit(cholesky)/cholesky | solution.py:85
  768.1 0.7 copy.25
  768.8 10.6 %custom-call.35 = f32[1,128,128]{1,2,0:T(8,128)} custom-call(f32[1,128,128]{2,1,0:T(8,128)S(1)} %get-tuple-element.44), custom_call_target="InvertDiagBlocksLowerTriangular" | custom-call | tf_op jit(solution)/shard_map/jit(cholesky)/cholesky | solution.py:85
  779.5 1.0 cholesky.225
  780.4 0.8 constant_dynamic-update-slice_fusion.1
  781.3 1.2 convolution_dynamic-update-slice_fusion
  782.5 0.6 convolution_subtract_fusion.7
  783.1 11.7 %cholesky.239 = f32[128,128]{1,0:T(8,128)S(1)} custom-call(f32[128,128]{1,0:T(8,128)S(1)} %cholesky.275), custom_call_target="Cholesky" | custom-call | tf_op jit(solution)/shard_map/jit(cholesky)/cholesky | solution.py:85
  794.9 9.8 %custom-call.36 = f32[1,128,128]{1,2,0:T(8,128)S(1)} custom-call(f32[1,128,128]{2,1,0:T(8,128)S(1)} %get-tuple-element.42), custom_call_target="InvertDiagBlocksLowerTriangular" | custom-call | tf_op jit(solution)/shard_map/jit(cholesky)/cholesky | solution.py:85
  805.5 11.9 %cholesky.256 = f32[128,128]{1,0:T(8,128)S(1)} custom-call(f32[128,128]{1,0:T(8,128)S(1)} %convolution_subtract_fusion.9), custom_call_target="Cholesky" | custom-call | tf_op jit(solution)/shard_map/jit(cholesky)/cholesky | solution.py:85
  817.6 0.6 compare_reduce_fusion.3
  818.3 0.6 compare_reduce_fusion.2
  818.9 0.7 compare_reduce_fusion.1
  819.6 0.7 compare_reduce_fusion
  823.0 0.7 triangular_solve.124
  823.7 10.8 %while.1 = (s32[]{:T(128)}, f32[512,512]{0,1:T(8,128)S(1)}, s32[4,2]{0,1:T(2,128)S(1)}, f32[4,128,128]{2,1,0:T(8,128)}, s32[]{:T(128)}) while((s32[]{:T(128)}, f32[512,512]{0,1:T(8,128)S(1)}, s32[4,2]{0,1:T(2,128)S(1)}, f32[4,128,128]{2,1,0:T(8,128)}, s32[]{:T(128)}) %tuple.34), condition=%wide.while_cond, body=%wide.while_body.sunk | while | flops 2 | bytes 393329 | solution.py:87
  824.3 1.4 dynamic-slice.7
  825.8 0.6 bitcast_dynamic-update-slice_fusion.2
  827.0 1.4 dynamic-slice.7
  828.5 0.6 bitcast_dynamic-update-slice_fusion.2
  829.7 1.4 dynamic-slice.7
  831.1 0.6 bitcast_dynamic-update-slice_fusion.2
  832.4 1.4 dynamic-slice.7
  833.8 0.6 bitcast_dynamic-update-slice_fusion.2
  834.5 40.8 %custom-call.37 = f32[4,128,128]{1,2,0:T(8,128)} custom-call(f32[4,128,128]{2,1,0:T(8,128)} %get-tuple-element.9), custom_call_target="InvertDiagBlocksLowerTriangular" | custom-call | tf_op jit(solution)/shard_map/jit(_solve_triangular)/triangular_solve | solution.py:87
  875.3 1.4 fusion.82
  876.7 1.2 fusion.93
  878.0 1.2 convolution_subtract_fusion.8
  879.2 1.1 fusion.113
  880.3 1.3 convolution_subtract_fusion.6
  881.7 1.2 fusion.115
  882.9 1.4 convolution_subtract_fusion.5
  884.3 1.1 fusion.117
  885.5 0.7 copy-done.9
  886.2 0.8 fusion.81
  887.0 2.0 copy.32
  889.6 1.3 fusion.112
  890.9 1.0 convolution_subtract_fusion.1
  891.9 1.3 fusion.114
  893.2 1.5 convolution_subtract_fusion.3
  894.7 1.3 fusion.116
  896.0 1.9 convolution_subtract_fusion
  897.8 1.0 copy.33
  (76 shorter events, 6.8 us)
Async XLA Ops:
  7.2 1.6 copy-start
  7.2 149.0 %all-reduce.7.cloned.1.call-start = ((), (), s32[]{:S(2)}) async-start(), calls=%async_computation.1 | async-start | bytes 2097152 | tf_op jit(solution)/shard_map/psum | solution.py:63
  20.5 189.2 %all-gather.2.cloned.1.call-start = ((), (), s32[]{:S(2)}) async-start(), calls=%async_computation.2 | async-start | bytes 2621440 | tf_op jit(solution)/shard_map/all_gather | solution.py:67
  158.3 53.9 %copy-start.1 = (bf16[128,2048]{1,0:T(8,128)(2,1)S(1)}, bf16[128,2048]{1,0:T(8,128)(2,1)}, u32[]{:S(2)}) copy-start(bf16[128,2048]{1,0:T(8,128)(2,1)} %multiply_convert_fusion) | copy-start | bytes 1572868
  158.3 118.5 %reduce-scatter.2.cloned.1.call-start = ((), (), s32[]{:S(2)}) async-start(), calls=%async_computation.3 | async-start | bytes 4718592 | tf_op jit(solution)/shard_map/reduce_scatter | solution.py:75
  214.9 363.3 %all-reduce.9.cloned.1.call-start = ((), (), s32[]{:S(2)}) async-start(), calls=%async_computation.4 | async-start | bytes 2097152 | tf_op jit(solution)/shard_map/psum | solution.py:14
  279.3 451.0 %all-reduce.11.cloned.1.call-start = ((), (), s32[]{:S(2)}) async-start(), calls=%async_computation.5 | async-start | bytes 3145728 | tf_op jit(solution)/shard_map/psum | solution.py:14
  823.0 66.0 %copy-start.2 = (f32[256,512]{0,1:T(8,128)S(1)}, f32[256,512]{0,1:T(8,128)}, u32[]{:S(2)}) copy-start(f32[256,512]{0,1:T(8,128)} %get-tuple-element.31) | copy-start | bytes 1572868
  834.5 56.4 %copy-start.3 = (f32[256,512]{0,1:T(8,128)S(1)}, f32[256,512]{0,1:T(8,128)}, u32[]{:S(2)}) copy-start(f32[256,512]{0,1:T(8,128)} %get-tuple-element.30) | copy-start | bytes 1572868
  880.3 5.1 copy-start.4
  882.8 2.6 copy-start.6
  885.5 0.7 copy-start.9
  889.0 6.9 copy-start.5
  889.0 6.9 copy-start.7
  889.0 6.9 copy-start.8
  889.0 6.9 copy-start.10
Sparse Core Ops, SparseCore 0:
  20.7 135.5 all-reduce.6
  158.9 50.7 all-gather.1
  215.1 61.7 reduce-scatter.1
  280.3 297.9 all-reduce.8
  581.1 149.0 all-reduce.10
where the time goes:
time: 915 us; the launch traced here: 906 us
  waiting for transfers between devices  696 us (76%)
  other arithmetic  131 us (14%)
  matrix products  35.4 us (4%)
  local copies, waits for them, and re-layouts  23.7 us (3%)
  between operations  18.7 us (2%)
    psum x2, waiting for transfers between devices, from_root(): return lax.psum(kept, axis)  448 us
    psum x1, waiting for transfers between devices, shards(): summed = lax.psum(projected, 'tp')  136 us
    another operation x15, other arithmetic, shards(): factor = jnp.linalg.cholesky(diag_block)  80.2 us
    reduce_scatter x1, waiting for transfers between devices, shards(): lax.psum_scatter(contract_rows(phi_columns, phi_rows), 'ex', scatter_dime...  61.2 us
    all_gather x1, waiting for transfers between devices, shards(): gathered = lax.all_gather(phi_columns, 'blk', axis=1, tiled=True)  51.3 us
    another operation x3, other arithmetic, shards(): jax.scipy.linalg.solve_triangular(factor, first_tile.T, lower=True)  41.5 us
  transfers between devices with their start and end apart: 5, of which 5 were waited for; matrix products, arithmetic and copies ran while one was open for 0% of the time, Pallas kernels for 0%

commit v1 on v0

v1 whole, which is shorter than its diff:
```python
import math

import jax
import jax.numpy as jnp
from jax import lax
from jax.experimental import pallas as pl
from jax.experimental.pallas import tpu as pltpu
from jax.sharding import PartitionSpec as P

SB = 128
EX, TP, BLK = 8, 16, 4
CHIPS = TP // 2
K, GDIM, EXAMPLES, PANEL = 8192, 32768, 1024, 512
HI = lax.Precision.HIGHEST
NT = (((1,), (1,)), ((), ()))
TN = (((0,), (0,)), ((), ()))
NN = (((1,), (0,)), ((), ()))


def wrap(value):
    value &= 0xFFFFFFFF
    return value - (1 << 32) if value >= (1 << 31) else value


C1, C2, C3 = -1640531535, 668265263, -2048144789
C4 = wrap(-1028477387 << 8)


def slot_of(b):
    return 2 * (b % 2) + b // 2


def right_shift(value, amount):
    return lax.shift_right_logical(value, jnp.full_like(value, amount))


def project_kernel(seed_ref, grads_ref, sel_ref, out_ref, chosen_ref, cvec_ref, sign_ref):
    block = pl.program_id(0)
    pool, coords = grads_ref.shape

    @pl.when(block == 0)
    def _():
        hot = (lax.broadcasted_iota(jnp.int32, (pool, SB), 0) == sel_ref[...]).astype(jnp.float32)
        hot = hot.astype(jnp.bfloat16)
        for s in range(coords // 256):
            chosen_ref[pl.ds(s * 256, 256), :] = lax.dot_general(
                grads_ref[:, s * 256 : (s + 1) * 256], hot, TN, preferred_element_type=jnp.float32
            ).astype(jnp.bfloat16)
        first_coord = lax.axis_index("tp") * coords
        cvec_ref[...] = (first_coord + lax.broadcasted_iota(jnp.int32, (8, coords), 1)) * jnp.int32(
            C1
        ) + seed_ref[0]

    first = block * PANEL + slot_of(lax.axis_index("blk")) * SB

    def rows(r, carry):
        ids = first + r * 16 + lax.broadcasted_iota(jnp.int32, (8, 128), 0)
        low = ids * jnp.int32(C2)
        high = low + jnp.int32(wrap(8 * C2))
        start = pl.multiple_of(r * 16, 16)
        for s in range(coords // 128):
            c = cvec_ref[:, s * 128 : (s + 1) * 128]
            halves = []
            for f in (low, high):
                h = c + f
                h = (h ^ right_shift(h, 16)) * jnp.int32(C3)
                h = (h ^ right_shift(h, 13)) * jnp.int32(C4)
                h = h ^ (h << 16)
                halves.append(jnp.where(h < 0, jnp.float32(-1), jnp.float32(1)))
            sign_ref[pl.ds(start, 16), s * 128 : (s + 1) * 128] = jnp.concatenate(halves, axis=0).astype(
                jnp.bfloat16
            )
        return carry

    lax.fori_loop(0, SB // 16, rows, 0)
    out_ref[0] = jnp.dot(sign_ref[...], chosen_ref[...], preferred_element_type=jnp.float32).astype(out_ref.dtype)


def project(seed, grads, sel):
    pool, coords = grads.shape
    return pl.pallas_call(
        project_kernel,
        grid=(TP,),
        out_shape=jax.ShapeDtypeStruct((TP, SB, SB), jnp.bfloat16),
        in_specs=[
            pl.BlockSpec(memory_space=pltpu.SMEM),
            pl.BlockSpec(grads.shape, lambda i: (0, 0)),
            pl.BlockSpec((1, SB), lambda i: (0, 0)),
        ],
        out_specs=pl.BlockSpec((1, SB, SB), lambda i: (i, 0, 0)),
        scratch_shapes=[
            pltpu.VMEM((coords, SB), jnp.bfloat16),
            pltpu.VMEM((8, coords), jnp.int32),
            pltpu.VMEM((SB, coords), jnp.bfloat16),
        ],
        name="project",
    )(seed, grads, sel)


def exchange_kernel(
    parts, fp, fr, fc, prx, rx,
    ps, pr, ms, mr, pys, pyr, mys, myr, rps, rpr, pzs, pzr,
    rs_, rr_, ls_, lr_, ras, rar, rds, rdr, pas, par, pds, pdr, loc,
):
    z, t, b = lax.axis_index("ex"), lax.axis_index("tp"), lax.axis_index("blk")
    u, c = t // 2, t % 2
    slot = slot_of(b)
    scaling = jnp.float32(1.0 / math.sqrt(GDIM))
    pending = []

    def to(**axes):
        at = {"ex": z, "tp": t, "blk": b}
        at.update(axes)
        return (at["ex"], at["tp"], at["blk"])

    def copy(src, dst, send, recv, target):
        return pltpu.make_async_remote_copy(
            src_ref=src, dst_ref=dst, send_sem=send, recv_sem=recv,
            device_id=target, device_id_type=pl.DeviceIdType.MESH,
        )

    def go(src, dst, send, recv, target):
        one = copy(src, dst, send, recv, target)
        one.start()
        pending.append(one)
        return one

    def lanes(index):
        return pl.ds(pl.multiple_of(index * SB, SB), SB)

    tp_peers = [(d, lax.rem(t + d, TP)) for d in range(1, TP)]
    chip_peers = [(d, lax.rem(u + d, CHIPS) * 2 + c) for d in range(1, CHIPS)]
    blk_peers = [(d, lax.rem(b + d, BLK)) for d in range(1, BLK)]
    ex_peers = [(d, lax.rem(z + d, EX)) for d in range(1, EX)]
    other = u * 2 + 1 - c
    mate = to(ex=u, tp=2 * z + b // 2, blk=2 * c + b % 2)
    alone = jnp.logical_and(u == z, b // 2 == c)

    barrier = pltpu.get_barrier_semaphore()

    def greet(target):
        pl.semaphore_signal(barrier, inc=1, device_id=target, device_id_type=pl.DeviceIdType.MESH)

    for _, p in tp_peers:
        greet(to(tp=p))
    for _, p in blk_peers:
        greet(to(blk=p))
    for _, p in ex_peers:
        greet(to(ex=p))

    @pl.when(jnp.logical_not(alone))
    def _():
        greet(mate)

    greeted = len(tp_peers) + len(blk_peers) + len(ex_peers) + 1
    pl.semaphore_wait(barrier, greeted - alone.astype(jnp.int32))

    panel_in, main_in = [], []
    for d, p in tp_peers:
        rows = pl.ds(pl.multiple_of((p // 2) * 16, 16), 16)
        panel_in.append(go(parts.at[0, rows, :], prx.at[d], ps.at[d], pr.at[d], to(tp=p)))
    for d, p in tp_peers:
        main_in.append(go(parts.at[p], rx.at[d], ms.at[d], mr.at[d], to(tp=p)))
    for one in panel_in:
        one.wait_recv()
    total = parts[0, pl.ds(pl.multiple_of(u * 16, 16), 16), :].astype(jnp.float32)
    for d in range(1, TP):
        total = total + prx[d].astype(jnp.float32)
    fp[slot, u, :, lanes(z)] = (total * scaling).astype(jnp.bfloat16)
    mine = fp.at[slot, u, :, lanes(z)]
    panel_y = [go(mine, mine, pys.at[d], pyr.at[d], to(blk=p)) for d, p in blk_peers]

    for one in main_in:
        one.wait_recv()
    total = parts[t].astype(jnp.float32)
    for d in range(1, TP):
        total = total + rx[d].astype(jnp.float32)
    fc[lanes(slot), lanes(z)] = (total * scaling).astype(jnp.bfloat16)
    mine = fc.at[lanes(slot), lanes(z)]
    main_y = [None] + [go(mine, mine, mys.at[d], myr.at[d], to(blk=p)) for d, p in blk_peers]

    row_slot = fr.at[lanes(b // 2), lanes(z)]
    moved = copy(mine, row_slot, rps, rpr, mate)

    @pl.when(alone)
    def _():
        pltpu.make_async_copy(mine, row_slot, loc).start()

    @pl.when(jnp.logical_not(alone))
    def _():
        moved.start()

    right, left = to(ex=lax.rem(z + 1, EX)), to(ex=lax.rem(z + EX - 1, EX))
    rights, lefts = {}, {}

    def piece(step, j):
        row = slot_of(lax.rem(b + BLK - j, BLK))
        return fc.at[lanes(row), lanes(lax.rem(z + step + EX, EX))]

    def pass_right(s, j):
        at = piece(-s, j)
        rights[s, j] = go(at, at, rs_.at[s, j], rr_.at[s, j], right)

    def pass_left(s, j):
        at = piece(s, j)
        lefts[s, j] = go(at, at, ls_.at[s, j], lr_.at[s, j], left)

    for j in range(BLK):
        if j:
            main_y[j].wait_recv()
        pass_right(0, j)
        pass_left(0, j)

    for one in panel_y:
        one.wait_recv()
    mine = fp.at[:, u, :, lanes(z)]
    panel_z = [go(mine, mine, pzs.at[d], pzr.at[d], to(ex=p)) for d, p in ex_peers]

    @pl.when(alone)
    def _():
        pltpu.make_async_copy(piece(0, 0), row_slot, loc).wait()

    @pl.when(jnp.logical_not(alone))
    def _():
        moved.wait_send()
        moved.wait_recv()

    def row_at(chip):
        return fr.at[lanes(c), lanes(chip)]

    mine = row_at(u)
    rows_in = [go(mine, mine, ras.at[d], rar.at[d], to(tp=p)) for d, p in chip_peers]
    rows_over = [go(mine, mine, rds.at[0], rdr.at[0], to(tp=other))]

    for one in panel_z:
        one.wait_recv()

    def panel_at(chip):
        return fp.at[pl.ds(2 * c, 2), chip]

    mine = panel_at(u)
    panel_a = [go(mine, mine, pas.at[d], par.at[d], to(tp=p)) for d, p in chip_peers]

    for s in range(1, EX // 2):
        for j in range(BLK):
            rights[s - 1, j].wait_recv()
            if s < EX // 2 - 1 or j < BLK // 2:
                pass_right(s, j)
            lefts[s - 1, j].wait_recv()
            if s < EX // 2 - 1 or j >= BLK // 2:
                pass_left(s, j)

    for d in range(1, CHIPS):
        rows_in[d - 1].wait_recv()
        at = row_at(lax.rem(u + CHIPS - d, CHIPS))
        rows_over.append(go(at, at, rds.at[d], rdr.at[d], to(tp=other)))
    panel_over = []
    for d in range(1, CHIPS):
        panel_a[d - 1].wait_recv()
        at = panel_at(lax.rem(u + CHIPS - d, CHIPS))
        panel_over.append(go(at, at, pds.at[d], pdr.at[d], to(tp=other)))
    last = EX // 2 - 1
    for j in range(BLK // 2):
        rights[last, j].wait_recv()
        lefts[last, BLK // 2 + j].wait_recv()
    for one in rows_over + panel_over:
        one.wait_recv()
    for one in pending:
        one.wait_send()


def exchange(parts):
    bf = jnp.bfloat16
    dma = pltpu.SemaphoreType.DMA
    sems = []
    for n in (TP, TP, BLK, BLK):
        sems += [dma((n,)), dma((n,))]
    sems += [dma, dma, dma((EX,)), dma((EX,))]
    sems += [dma((EX // 2, BLK))] * 4
    sems += [dma((CHIPS,))] * 8
    sems += [dma]
    vmem = pl.BlockSpec(memory_space=pltpu.VMEM)
    return pl.pallas_call(
        exchange_kernel,
        out_shape=(
            jax.ShapeDtypeStruct((BLK, CHIPS, 16, EXAMPLES), bf),
            jax.ShapeDtypeStruct((2 * SB, EXAMPLES), bf),
            jax.ShapeDtypeStruct((PANEL, EXAMPLES), bf),
        ),
        in_specs=[vmem],
        out_specs=(vmem, vmem, vmem),
        scratch_shapes=[pltpu.VMEM((TP, 16, SB), bf), pltpu.VMEM((TP, SB, SB), bf)] + sems,
        compiler_params=pltpu.CompilerParams(collective_id=0, has_side_effects=True),
        name="exchange",
    )(parts)


def split3(x):
    a = x.astype(jnp.bfloat16)
    r = x - a.astype(jnp.float32)
    b = r.astype(jnp.bfloat16)
    c = (r - b.astype(jnp.float32)).astype(jnp.bfloat16)
    return a, b, c

def dot3(x, y, dims):
    xa, xb, xc = split3(x)
    ya, yb, yc = split3(y)
    kx, ky = dims[0][0][0], dims[0][1][0]
    left = jnp.concatenate([xa, xa, xb, xa, xb, xc], axis=kx)
    right = jnp.concatenate([ya, yb, ya, yc, yb, ya], axis=ky)
    return lax.dot_general(left, right, dims, preferred_element_type=jnp.float32)

def base_inverse(s):
    n = 128
    rowid = lax.broadcasted_iota(jnp.int32, (8, 128), 0)
    lane = lax.broadcasted_iota(jnp.int32, (8, 128), 1)
    top = [s[8 * i:8 * i + 8, :] for i in range(n // 8)]
    aug = [(lane == rowid + 8 * i).astype(jnp.float32) for i in range(n // 8)]
    done = []
    for m in range(n // 8):
        r, a = top[m], aug[m]
        v = [jnp.broadcast_to(r[:, 8 * m + k:8 * m + k + 1], (8, 128)) for k in range(8)]
        scale = jnp.zeros((8, 128), jnp.float32)
        for j in range(8):
            d = jnp.broadcast_to(v[j][j:j + 1, :], (8, 128))
            scale = jnp.where(rowid == j, lax.rsqrt(d), scale)
            if j < 7:
                f = jnp.where(rowid > j, v[j] / d, 0.0)
                for k in range(j + 1, 8):
                    v[k] = v[k] - f * jnp.broadcast_to(v[k][j:j + 1, :], (8, 128))
                r = r - f * jnp.broadcast_to(r[j:j + 1, :], (8, 128))
                a = a - f * jnp.broadcast_to(a[j:j + 1, :], (8, 128))
        r = r * scale
        a = a * scale
        done.append(a)
        if m < n // 8 - 1:
            ra, rb, rc = split3(r)
            aa, ab, ac = split3(a)
            lo = 8 * (m + 1)
            left = jnp.concatenate([ra, ra, rb, ra, rb, rc], axis=0)
            right = jnp.concatenate([jnp.concatenate([x, y], axis=1) for x, y in
                                     ((ra, aa), (rb, ab), (ra, aa), (rc, ac), (rb, ab), (ra, aa))], axis=0)
            u = lax.dot_general(left, right, TN, preferred_element_type=jnp.float32)
            for i in range(m + 1, n // 8):
                top[i] = top[i] - u[8 * i:8 * i + 8, :128]
                aug[i] = aug[i] - u[8 * i:8 * i + 8, 128:]
    return jnp.concatenate(done, axis=0)

def factor_inverse(A, N, M):
    for k in range(4):
        rk = slice(128 * k, 128 * k + 128)
        w = base_inverse(A[rk, rk])
        if k > 0:
            M[rk, :128 * k] = dot3(w, N[rk, :128 * k], (((1,), (0,)), ((), ())))
        M[rk, rk] = w
        if k < 3:
            M[rk, 128 * (k + 1):] = jnp.zeros((128, 512 - 128 * (k + 1)), jnp.float32)
            y = dot3(w, A[rk, 128 * (k + 1):], (((1,), (0,)), ((), ())))
            ym = M[rk, :128 * (k + 1)]
            for i in range(k + 1, 4):
                ri = slice(128 * i, 128 * i + 128)
                yi = y[:, 128 * (i - k - 1):128 * (i - k)]
                A[ri, 128 * i:] = A[ri, 128 * i:] - dot3(yi, y[:, 128 * (i - k - 1):], TN)
                up = dot3(yi, ym, TN)
                if k > 0:
                    N[ri, :128 * k] = N[ri, :128 * k] - up[:, :128 * k]
                N[ri, rk] = -up[:, 128 * k:]

def final_kernel(ridge, fp, fr, fc, pan, trail, A, N, M, X):
    inv = jnp.float32(1.0 / fp.shape[1])
    g, t = lax.axis_index("ex") * BLK + lax.axis_index("blk"), lax.axis_index("tp")
    rv = ridge[0]
    def diag(shape, r0, c0):
        return jnp.where(lax.broadcasted_iota(jnp.int32, shape, 0) + r0 == lax.broadcasted_iota(jnp.int32, shape, 1) + c0, rv, 0.0)
    A[...] = lax.dot_general(fp[...], fp[...], NT, preferred_element_type=jnp.float32) * inv + diag((512, 512), 0, 0)
    factor_inverse(A, N, M)
    A[...] = lax.dot_general(fp[...], fc[...], NT, preferred_element_type=jnp.float32) * inv + diag((512, 512), 0, t * 512)
    X[...] = jnp.dot(M[...], A[...], precision=HI)
    N[:256] = lax.dot_general(fr[...], fp[...], NT, preferred_element_type=jnp.float32) * inv + diag((256, 512), g * 256, 0)
    pan[...] = lax.dot_general(N[:256], M[...], NT, precision=HI)
    own = lax.dot_general(fr[...], fc[...], NT, preferred_element_type=jnp.float32) * inv + diag((256, 512), g * 256, t * 512)
    trail[...] = own - jnp.dot(pan[...], X[...], precision=HI)

def finish(ridge, fp, fr, fc):
    return pl.pallas_call(
        final_kernel,
        out_shape=(jax.ShapeDtypeStruct((256, 512), jnp.float32), jax.ShapeDtypeStruct((256, 512), jnp.float32)),
        in_specs=[pl.BlockSpec(memory_space=pltpu.SMEM)] + [pl.BlockSpec(memory_space=pltpu.VMEM)] * 3,
        out_specs=(pl.BlockSpec(memory_space=pltpu.VMEM),) * 2,
        scratch_shapes=[pltpu.VMEM((512, 512), jnp.float32)] * 4,
        name="finish",
    )(ridge, fp, fr, fc)


def shards(gradients, selection, seed_value, ridge_value):
    parts = project(seed_value, gradients, selection.reshape(1, SB))
    fp, fr, fc = exchange(parts)
    return finish(ridge_value, fp.reshape(PANEL, EXAMPLES), fr, fc)


def solution(mesh):
    in_specs = (P("ex", "tp"), P("ex"), P(), P())
    out_specs = (P(("ex", "blk"), None), P(("ex", "blk"), "tp"))
    return jax.shard_map(shards, mesh=mesh, in_specs=in_specs, out_specs=out_specs, check_vma=False)
```

time: 915 us -> 104 us (0.11); the launches traced: 906 us -> 104 us
  waiting for transfers between devices: 696 us -> 0 us
  other arithmetic: 131 us -> 0 us
  Pallas kernels: 0 us -> 102 us
  matrix products: 35.4 us -> 0 us
  local copies, waits for them, and re-layouts: 23.7 us -> 0 us
  between operations: 18.7 us -> 1.93 us
    psum x3 -> x0, waiting for transfers between devices: 583 us -> none  [the longest x2 448 us: from_root(): return lax.psum(kept, axis)]
    another operation x18 -> x0, other arithmetic: 122 us -> none  [the longest x15 80.2 us: shards(): factor = jnp.linalg.cholesky(diag_block)]
    pallas_call x0 -> x3, Pallas kernels: none -> 102 us  [the longest x1 54.1 us: exchange(): pl.pallas_call(exchange_kernel, out_shape=(jax.ShapeDtypeStruct((BLK, CHI...]
    reduce_scatter x1 -> x0, waiting for transfers between devices: 61.2 us -> none  [shards(): lax.psum_scatter(contract_rows(phi_columns, phi_rows), 'ex', scatter_dime...]
    all_gather x1 -> x0, waiting for transfers between devices: 51.3 us -> none  [shards(): gathered = lax.all_gather(phi_columns, 'blk', axis=1, tiled=True)]
    another operation x20 -> x0, matrix products: 20.1 us -> none  [the longest x7 8.7 us: shards(): jax.scipy.linalg.solve_triangular(factor, first_tile.T, lower=True)]
    dot_general x6 -> x0, matrix products: 15.3 us -> none  [the longest x4 10.8 us: shards(): jnp.dot(chosen[:, segment * stride:(segment + 1) * stride], sign_values,...]
    another operation x34 -> x0, local copies, waits for them, and re-layouts: 15 us -> none
  transfers between devices with their start and end apart: 5 -> 0, of which waited for: 5 -> 0; matrix products, arithmetic and copies ran while one was open for 0% -> 0% of each run, Pallas kernels for 0% -> 0%
where the time goes in v1:
time: 104 us
  Pallas kernels  102 us (98%)
  between operations  1.93 us (2%)
    pallas_call x1, Pallas kernels, exchange(): pl.pallas_call(exchange_kernel, out_shape=(jax.ShapeDtypeStruct((BLK, CHI...  54.1 us
    pallas_call x1, Pallas kernels, finish(): pl.pallas_call(final_kernel, out_shape=(jax.ShapeDtypeStruct((256, 512),...  33 us
    pallas_call x1, Pallas kernels, project(): pl.pallas_call(project_kernel, grid=(TP,), out_shape=jax.ShapeDtypeStruct...  15.1 us

profile of v1, /device:TPU:1, one launch (start us, length us, event | category | flops | bytes accessed | tf_op | source)
XLA Modules:
  0.0 104.1 jit_solution(3201703279860470318)
XLA Ops:
  1.9 15.1 %project.1.parts = bf16[16,128,128]{2,1,0:T(8,128)(2,1)} custom-call(s32[1]{0:T(128)S(6)} %copy.6.seed_ref, bf16[256,2048]{1,0:T(8,128)(2,1)} %grads_ref.1, s32[1,128]{1,0:T(1,128)} %bitcast.3), custom_call_target="tpu_custom_call" | custom-call | tf_op jit(solution)/shard_map/project/pallas_call | solution.py:81
  17.1 54.1 %exchange.1 = (bf16[4,8,16,1024]{3,2,1,0:T(8,128)(2,1)}, bf16[256,1024]{1,0:T(8,128)(2,1)}, bf16[512,1024]{1,0:T(8,128)(2,1)}) custom-call(bf16[16,128,128]{2,1,0:T(8,128)(2,1)} %project.1.parts), custom_call_target="tpu_custom_call" | custom-call | tf_op jit(solution)/shard_map/exchange/pallas_call | solution.py:283
  71.1 33.0 %finish.1 = (f32[256,512]{1,0:T(8,128)}, f32[256,512]{1,0:T(8,128)}) custom-call(f32[1]{0:T(128)S(6)} %copy.7.ridge, bf16[512,1024]{1,0:T(8,128)(2,1)} %bitcast.2, bf16[256,1024]{1,0:T(8,128)(2,1)} %get-tuple-element.6.fr, bf16[512,1024]{1,0:T(8,128)(2,1)} %get-tuple-element.7.fc), custom_call_target="tpu_custom_call" | custom-call | tf_op jit(solution)/shard_map/finish/pallas_call | solution.py:385

commit v2 on v0

v2 whole, which is shorter than its diff:
```python
import math

import jax
import jax.numpy as jnp
from jax import lax
from jax.experimental import pallas as pl
from jax.experimental.pallas import tpu as pltpu
from jax.sharding import PartitionSpec as P

SB = 128
EX, TP, BLK = 8, 16, 4
CHIPS = TP // 2
K, GDIM, EXAMPLES, PANEL = 8192, 32768, 1024, 512
HI = lax.Precision.HIGHEST
NT = (((1,), (1,)), ((), ()))
TN = (((0,), (0,)), ((), ()))
NN = (((1,), (0,)), ((), ()))


def wrap(value):
    value &= 0xFFFFFFFF
    return value - (1 << 32) if value >= (1 << 31) else value


C1, C2, C3 = -1640531535, 668265263, -2048144789
CUT1, CUT2, CUT3 = 5, 9, 13
C4 = wrap(-1028477387 << 8)


def slot_of(b):
    return 2 * (b % 2) + b // 2


def right_shift(value, amount):
    return lax.shift_right_logical(value, jnp.full_like(value, amount))


def split3(x):
    a = x.astype(jnp.bfloat16)
    r = x - a.astype(jnp.float32)
    b = r.astype(jnp.bfloat16)
    c = (r - b.astype(jnp.float32)).astype(jnp.bfloat16)
    return a, b, c

def dot3(x, y, dims):
    xa, xb, xc = split3(x)
    ya, yb, yc = split3(y)
    kx, ky = dims[0][0][0], dims[0][1][0]
    left = jnp.concatenate([xa, xa, xb, xa, xb, xc], axis=kx)
    right = jnp.concatenate([ya, yb, ya, yc, yb, ya], axis=ky)
    return lax.dot_general(left, right, dims, preferred_element_type=jnp.float32)

def base_inverse(s, hook):
    n = 128
    rowid = lax.broadcasted_iota(jnp.int32, (8, 128), 0)
    lane = lax.broadcasted_iota(jnp.int32, (8, 128), 1)
    top = [s[8 * i:8 * i + 8, :] for i in range(n // 8)]
    aug = [(lane == rowid + 8 * i).astype(jnp.float32) for i in range(n // 8)]
    done = []
    for m in range(n // 8):
        r, a = top[m], aug[m]
        v = [jnp.broadcast_to(r[:, 8 * m + k:8 * m + k + 1], (8, 128)) for k in range(8)]
        scale = jnp.zeros((8, 128), jnp.float32)
        for j in range(8):
            d = jnp.broadcast_to(v[j][j:j + 1, :], (8, 128))
            scale = jnp.where(rowid == j, lax.rsqrt(d), scale)
            if j < 7:
                f = jnp.where(rowid > j, v[j] / d, 0.0)
                for k in range(j + 1, 8):
                    v[k] = v[k] - f * jnp.broadcast_to(v[k][j:j + 1, :], (8, 128))
                r = r - f * jnp.broadcast_to(r[j:j + 1, :], (8, 128))
                a = a - f * jnp.broadcast_to(a[j:j + 1, :], (8, 128))
        r = r * scale
        a = a * scale
        done.append(a)
        hook(m)
        if m < n // 8 - 1:
            ra, rb, rc = split3(r)
            aa, ab, ac = split3(a)
            lo = 8 * (m + 1)
            left = jnp.concatenate([ra, ra, rb, ra, rb, rc], axis=0)
            right = jnp.concatenate([jnp.concatenate([x, y], axis=1) for x, y in
                                     ((ra, aa), (rb, ab), (ra, aa), (rc, ac), (rb, ab), (ra, aa))], axis=0)
            u = lax.dot_general(left, right, TN, preferred_element_type=jnp.float32)
            for i in range(m + 1, n // 8):
                top[i] = top[i] - u[8 * i:8 * i + 8, :128]
                aug[i] = aug[i] - u[8 * i:8 * i + 8, 128:]
    return jnp.concatenate(done, axis=0)

def factor_inverse(A, N, M, hook):
    for k in range(4):
        rk = slice(128 * k, 128 * k + 128)
        w = base_inverse(A[rk, rk], lambda m, k=k: hook(k, m))
        if k > 0:
            M[rk, :128 * k] = dot3(w, N[rk, :128 * k], (((1,), (0,)), ((), ())))
        M[rk, rk] = w
        if k < 3:
            M[rk, 128 * (k + 1):] = jnp.zeros((128, 512 - 128 * (k + 1)), jnp.float32)
            y = dot3(w, A[rk, 128 * (k + 1):], (((1,), (0,)), ((), ())))
            ym = M[rk, :128 * (k + 1)]
            for i in range(k + 1, 4):
                ri = slice(128 * i, 128 * i + 128)
                yi = y[:, 128 * (i - k - 1):128 * (i - k)]
                A[ri, 128 * i:] = A[ri, 128 * i:] - dot3(yi, y[:, 128 * (i - k - 1):], TN)
                up = dot3(yi, ym, TN)
                if k > 0:
                    N[ri, :128 * k] = N[ri, :128 * k] - up[:, :128 * k]
                N[ri, rk] = -up[:, 128 * k:]


def split2(x):
    a = x.astype(jnp.bfloat16)
    return a, (x - a.astype(jnp.float32)).astype(jnp.bfloat16)


def dot2(x, y, dims):
    xa, xb = split2(x)
    ya, yb = split2(y)

    def one(p, q):
        return lax.dot_general(p, q, dims, preferred_element_type=jnp.float32)

    return one(xa, ya) + (one(xa, yb) + one(xb, ya))


def whole_kernel(
    seed_ref, ridge_ref, grads_ref, sel_ref, pan, trail,
    chosen_ref, cvec_ref, sign_ref, parts, fp, fr, fc, prx, rx, A, N, M, X,
    ps, pr, ms, mr, pys, pyr, mys, myr, rps, rpr, pzs, pzr,
    rs_, rr_, ls_, lr_, ras, rar, rds, rdr, pas, par, pds, pdr, loc,
):
    z, t, b = lax.axis_index("ex"), lax.axis_index("tp"), lax.axis_index("blk")
    u, c = t // 2, t % 2
    slot = slot_of(b)
    scaling = jnp.float32(1.0 / math.sqrt(GDIM))
    pool, coords = grads_ref.shape
    pending = []

    def to(**axes):
        at = {"ex": z, "tp": t, "blk": b}
        at.update(axes)
        return (at["ex"], at["tp"], at["blk"])

    def copy(src, dst, send, recv, target):
        return pltpu.make_async_remote_copy(
            src_ref=src, dst_ref=dst, send_sem=send, recv_sem=recv,
            device_id=target, device_id_type=pl.DeviceIdType.MESH,
        )

    def go(src, dst, send, recv, target):
        one = copy(src, dst, send, recv, target)
        one.start()
        pending.append(one)
        return one

    def lanes(index):
        return pl.ds(pl.multiple_of(index * SB, SB), SB)

    tp_peers = [(d, lax.rem(t + d, TP)) for d in range(1, TP)]
    chip_peers = [(d, lax.rem(u + d, CHIPS) * 2 + c) for d in range(1, CHIPS)]
    blk_peers = [(d, lax.rem(b + d, BLK)) for d in range(1, BLK)]
    ex_peers = [(d, lax.rem(z + d, EX)) for d in range(1, EX)]
    other = u * 2 + 1 - c
    mate = to(ex=u, tp=2 * z + b // 2, blk=2 * c + b % 2)
    alone = jnp.logical_and(u == z, b // 2 == c)

    barrier = pltpu.get_barrier_semaphore()

    def greet(target):
        pl.semaphore_signal(barrier, inc=1, device_id=target, device_id_type=pl.DeviceIdType.MESH)

    for _, p in tp_peers:
        greet(to(tp=p))
    for _, p in blk_peers:
        greet(to(blk=p))
    for _, p in ex_peers:
        greet(to(ex=p))

    @pl.when(jnp.logical_not(alone))
    def _():
        greet(mate)

    hot = (lax.broadcasted_iota(jnp.int32, (pool, SB), 0) == sel_ref[...]).astype(jnp.float32)
    hot = hot.astype(jnp.bfloat16)
    for s in range(coords // 256):
        chosen_ref[pl.ds(s * 256, 256), :] = lax.dot_general(
            grads_ref[:, s * 256 : (s + 1) * 256], hot, TN, preferred_element_type=jnp.float32
        ).astype(jnp.bfloat16)
    cvec_ref[...] = (t * coords + lax.broadcasted_iota(jnp.int32, (8, coords), 1)) * jnp.int32(C1) + seed_ref[0]

    def product(block):
        first = block * PANEL + slot * SB

        def rows(r, carry):
            ids = first + r * 16 + lax.broadcasted_iota(jnp.int32, (8, 128), 0)
            low = ids * jnp.int32(C2)
            high = low + jnp.int32(wrap(8 * C2))
            start = pl.multiple_of(r * 16, 16)
            for s in range(coords // 128):
                at = cvec_ref[:, s * 128 : (s + 1) * 128]
                halves = []
                for f in (low, high):
                    h = at + f
                    h = (h ^ right_shift(h, 16)) * jnp.int32(C3)
                    h = (h ^ right_shift(h, 13)) * jnp.int32(C4)
                    h = h ^ (h << 16)
                    halves.append(jnp.where(h < 0, jnp.float32(-1), jnp.float32(1)))
                sign_ref[pl.ds(start, 16), s * 128 : (s + 1) * 128] = jnp.concatenate(halves, axis=0).astype(
                    jnp.bfloat16
                )
            return carry

        lax.fori_loop(0, SB // 16, rows, 0)
        out = jnp.dot(sign_ref[...], chosen_ref[...], preferred_element_type=jnp.float32)
        parts[block] = out.astype(jnp.bfloat16)

    product(0)
    greeted = len(tp_peers) + len(blk_peers) + len(ex_peers) + 1
    pl.semaphore_wait(barrier, greeted - alone.astype(jnp.int32))

    panel_in = []
    for d, p in tp_peers:
        rows16 = pl.ds(pl.multiple_of((p // 2) * 16, 16), 16)
        panel_in.append(go(parts.at[0, rows16, :], prx.at[d], ps.at[d], pr.at[d], to(tp=p)))

    def share(d):
        p = lax.rem(t + d, TP)
        return copy(parts.at[p], rx.at[d], ms.at[d], mr.at[d], to(tp=p))

    def blocks(lo, hi):
        def body(d, carry):
            p = lax.rem(t + d, TP)

            @pl.when(p != 0)
            def _():
                product(p)

            share(d).start()
            return carry

        lax.fori_loop(lo, hi, body, 0)

    blocks(1, CUT1)
    for one in panel_in:
        one.wait_recv()
    total = parts[0, pl.ds(pl.multiple_of(u * 16, 16), 16), :].astype(jnp.float32)
    for d in range(1, TP):
        total = total + prx[d].astype(jnp.float32)
    fp[slot, u, :, lanes(z)] = (total * scaling).astype(jnp.bfloat16)
    mine = fp.at[slot, u, :, lanes(z)]
    panel_y = [go(mine, mine, pys.at[d], pyr.at[d], to(blk=p)) for d, p in blk_peers]

    blocks(CUT1, CUT2)
    for one in panel_y:
        one.wait_recv()
    mine = fp.at[:, u, :, lanes(z)]
    panel_z = [go(mine, mine, pzs.at[d], pzr.at[d], to(ex=p)) for d, p in ex_peers]

    blocks(CUT2, CUT3)
    for one in panel_z:
        one.wait_recv()

    def panel_at(chip):
        return fp.at[pl.ds(2 * c, 2), chip]

    mine = panel_at(u)
    panel_a = [go(mine, mine, pas.at[d], par.at[d], to(tp=p)) for d, p in chip_peers]

    blocks(CUT3, TP)

    @pl.when(t != 0)
    def _():
        product(t)

    for d in range(1, TP):
        share(d).wait_recv()
    total = parts[t].astype(jnp.float32)
    for d in range(1, TP):
        total = total + rx[d].astype(jnp.float32)
    fc[lanes(slot), lanes(z)] = (total * scaling).astype(jnp.bfloat16)
    mine = fc.at[lanes(slot), lanes(z)]
    main_y = [None] + [go(mine, mine, mys.at[d], myr.at[d], to(blk=p)) for d, p in blk_peers]

    row_slot = fr.at[lanes(b // 2), lanes(z)]
    moved = copy(mine, row_slot, rps, rpr, mate)

    @pl.when(alone)
    def _():
        pltpu.make_async_copy(mine, row_slot, loc).start()

    @pl.when(jnp.logical_not(alone))
    def _():
        moved.start()

    right, left = to(ex=lax.rem(z + 1, EX)), to(ex=lax.rem(z + EX - 1, EX))
    rights, lefts = {}, {}

    def piece(step, j):
        row = slot_of(lax.rem(b + BLK - j, BLK))
        return fc.at[lanes(row), lanes(lax.rem(z + step + EX, EX))]

    def pass_right(s, j):
        at = piece(-s, j)
        rights[s, j] = go(at, at, rs_.at[s, j], rr_.at[s, j], right)

    def pass_left(s, j):
        at = piece(s, j)
        lefts[s, j] = go(at, at, ls_.at[s, j], lr_.at[s, j], left)

    pass_right(0, 0)
    pass_left(0, 0)

    panel_over = []
    for d in range(1, CHIPS):
        panel_a[d - 1].wait_recv()
        at = panel_at(lax.rem(u + CHIPS - d, CHIPS))
        panel_over.append(go(at, at, pds.at[d], pdr.at[d], to(tp=other)))
    for one in panel_over:
        one.wait_recv()

    def along_blk():
        for j in range(1, BLK):
            main_y[j].wait_recv()
            pass_right(0, j)
            pass_left(0, j)

    def row_at(chip):
        return fr.at[lanes(c), lanes(chip)]

    rows_in, rows_over = [], []

    def rows_out():
        @pl.when(alone)
        def _():
            pltpu.make_async_copy(piece(0, 0), row_slot, loc).wait()

        @pl.when(jnp.logical_not(alone))
        def _():
            moved.wait_send()
            moved.wait_recv()

        mine = row_at(u)
        rows_in.extend(go(mine, mine, ras.at[d], rar.at[d], to(tp=p)) for d, p in chip_peers)
        rows_over.append(go(mine, mine, rds.at[0], rdr.at[0], to(tp=other)))

    def ring(s, js):
        for j in js:
            rights[s - 1, j].wait_recv()
            if s < EX // 2 - 1 or j < BLK // 2:
                pass_right(s, j)
            lefts[s - 1, j].wait_recv()
            if s < EX // 2 - 1 or j >= BLK // 2:
                pass_left(s, j)

    def rows_across():
        for d in range(1, CHIPS):
            rows_in[d - 1].wait_recv()
            at = row_at(lax.rem(u + CHIPS - d, CHIPS))
            rows_over.append(go(at, at, rds.at[d], rdr.at[d], to(tp=other)))

    actions = {
        (0, 12): (along_blk, rows_out),
        (1, 2): (lambda: ring(1, (0,)),),
        (1, 7): (lambda: ring(1, (1,)),),
        (1, 11): (lambda: ring(1, (2,)),),
        (1, 15): (lambda: ring(1, (3,)), lambda: ring(2, (0,))),
        (2, 3): (lambda: ring(2, (1,)),),
        (2, 7): (lambda: ring(2, (2,)),),
        (2, 11): (lambda: ring(2, (3,)), lambda: ring(3, (0,))),
        (2, 15): (lambda: ring(3, (1,)),),
        (3, 3): (lambda: ring(3, (2,)),),
        (3, 7): (lambda: ring(3, (3,)), rows_across),
    }

    def hook(k, m):
        for act in actions.get((k, m), ()):
            act()

    g = z * BLK + b
    inv = jnp.float32(1.0 / EXAMPLES)
    rv = ridge_ref[0]

    def gram(left_part, right_part, r0, c0):
        out = lax.dot_general(left_part, right_part, NT, preferred_element_type=jnp.float32) * inv
        rows_, cols_ = (lax.broadcasted_iota(jnp.int32, out.shape, k) for k in range(2))
        return out + jnp.where(rows_ + r0 == cols_ + c0, rv, 0.0)

    panel = fp[...].reshape(PANEL, EXAMPLES)
    A[...] = gram(panel, panel, 0, 0)
    factor_inverse(A, N, M, hook)

    last = EX // 2 - 1
    for j in range(BLK // 2):
        rights[last, j].wait_recv()
        lefts[last, BLK // 2 + j].wait_recv()
    for one in rows_over:
        one.wait_recv()
    for one in pending:
        one.wait_send()
    for d in range(1, TP):
        share(d).wait_send()

    panel = fp[...].reshape(PANEL, EXAMPLES)
    X[...] = dot2(M[...], gram(panel, fc[...], 0, t * PANEL), NN)
    first_tile = gram(fr[...], panel, g * 2 * SB, 0)
    own = gram(fr[...], fc[...], g * 2 * SB, t * PANEL)
    out = dot2(first_tile, M[...], NT)
    pan[...] = out
    trail[...] = own - dot2(out, X[...], NN)


def whole(seed, ridge, grads, sel):
    bf, f32 = jnp.bfloat16, jnp.float32
    coords = grads.shape[1]
    dma = pltpu.SemaphoreType.DMA
    sems = []
    for n in (TP, TP, BLK, BLK):
        sems += [dma((n,)), dma((n,))]
    sems += [dma, dma, dma((EX,)), dma((EX,))]
    sems += [dma((EX // 2, BLK))] * 4
    sems += [dma((CHIPS,))] * 8
    sems += [dma]
    vmem = pl.BlockSpec(memory_space=pltpu.VMEM)
    smem = pl.BlockSpec(memory_space=pltpu.SMEM)
    tile = jax.ShapeDtypeStruct((2 * SB, PANEL), f32)
    square = pltpu.VMEM((PANEL, PANEL), f32)
    return pl.pallas_call(
        whole_kernel,
        out_shape=(tile, tile),
        in_specs=[smem, smem, vmem, vmem],
        out_specs=(vmem, vmem),
        scratch_shapes=[
            pltpu.VMEM((coords, SB), bf),
            pltpu.VMEM((8, coords), jnp.int32),
            pltpu.VMEM((SB, coords), bf),
            pltpu.VMEM((TP, SB, SB), bf),
            pltpu.VMEM((BLK, CHIPS, 16, EXAMPLES), bf),
            pltpu.VMEM((2 * SB, EXAMPLES), bf),
            pltpu.VMEM((PANEL, EXAMPLES), bf),
            pltpu.VMEM((TP, 16, SB), bf),
            pltpu.VMEM((TP, SB, SB), bf),
            square, square, square, square,
            *sems,
        ],
        compiler_params=pltpu.CompilerParams(collective_id=0, has_side_effects=True),
        name="whole",
    )(seed, ridge, grads, sel)


def shards(gradients, selection, seed_value, ridge_value):
    return whole(seed_value, ridge_value, gradients, selection.reshape(1, SB))


def solution(mesh):
    in_specs = (P("ex", "tp"), P("ex"), P(), P())
    out_specs = (P(("ex", "blk"), None), P(("ex", "blk"), "tp"))
    return jax.shard_map(shards, mesh=mesh, in_specs=in_specs, out_specs=out_specs, check_vma=False)
```

time: 915 us -> 80.3 us (0.09)
  waiting for transfers between devices: 696 us -> 0 us
  other arithmetic: 131 us -> 0 us
  Pallas kernels: 0 us -> 75.2 us
  matrix products: 35.4 us -> 0 us
  local copies, waits for them, and re-layouts: 23.7 us -> 2.72 us
  between operations: 18.7 us -> 1.94 us
    psum x3 -> x0, waiting for transfers between devices: 583 us -> none  [the longest x2 448 us: from_root(): return lax.psum(kept, axis)]
    another operation x18 -> x0, other arithmetic: 122 us -> none  [the longest x15 80.2 us: shards(): factor = jnp.linalg.cholesky(diag_block)]
    pallas_call x0 -> x1, Pallas kernels: none -> 75.2 us  [whole(): pl.pallas_call(whole_kernel, out_shape=(tile, tile), in_specs=[smem, smem...]
    reduce_scatter x1 -> x0, waiting for transfers between devices: 61.2 us -> none  [shards(): lax.psum_scatter(contract_rows(phi_columns, phi_rows), 'ex', scatter_dime...]
    all_gather x1 -> x0, waiting for transfers between devices: 51.3 us -> none  [shards(): gathered = lax.all_gather(phi_columns, 'blk', axis=1, tiled=True)]
    another operation x20 -> x0, matrix products: 20.1 us -> none  [the longest x7 8.7 us: shards(): jax.scipy.linalg.solve_triangular(factor, first_tile.T, lower=True)]
    dot_general x6 -> x0, matrix products: 15.3 us -> none  [the longest x4 10.8 us: shards(): jnp.dot(chosen[:, segment * stride:(segment + 1) * stride], sign_values,...]
    another operation x34 -> x0, local copies, waits for them, and re-layouts: 15 us -> none
  transfers between devices with their start and end apart: 5 -> 0, of which waited for: 5 -> 0; matrix products, arithmetic and copies ran while one was open for 0% -> 0% of each run, Pallas kernels for 0% -> 0%
where the time goes in v2:
time: 80.3 us; the launch traced here: 79.9 us
  Pallas kernels  75.2 us (94%)
  local copies, waits for them, and re-layouts  2.72 us (3%)
  between operations  1.94 us (2%)
    pallas_call x1, Pallas kernels, whole(): pl.pallas_call(whole_kernel, out_shape=(tile, tile), in_specs=[smem, smem...  75.2 us
    unnamed x4, local copies, waits for them, and re-layouts  2.72 us

profile of v2, /device:TPU:1, one launch (start us, length us, event | category | flops | bytes accessed | tf_op | source)
XLA Modules:
  0.0 79.9 jit_solution(18158718664192266608)
XLA Ops:
  1.9 75.2 %whole.1 = (f32[256,512]{1,0:T(8,128)}, f32[256,512]{1,0:T(8,128)}) custom-call(s32[1]{0:T(128)S(6)} %copy.8.seed_ref, f32[1]{0:T(128)S(6)} %copy.9.ridge_ref, bf16[256,2048]{1,0:T(8,128)(2,1)} %grads_ref.1, s32[1,128]{1,0:T(1,128)} %bitcast.1), custom_call_target="tpu_custom_call" | custom-call | tf_op jit(solution)/shard_map/whole/pallas_call | solution.py:427
  77.1 0.0 copy-start
  77.2 1.9 %copy.10 = f32[256,512]{1,0:T(8,128)} copy(f32[256,512]{1,0:T(8,128)} %get-tuple-element.4) | data formatting | bytes 1048576
  79.1 0.0 copy-done
  79.1 0.8 copy.11
Async XLA Ops:
  77.1 1.9 %copy-start = (f32[256,512]{1,0:T(8,128)S(1)}, f32[256,512]{1,0:T(8,128)}, u32[]{:S(2)}) copy-start(f32[256,512]{1,0:T(8,128)} %get-tuple-element.5) | copy-start | bytes 1572868

commit v3 on v2

--- a/solution.py
+++ b/solution.py
@@ -23,7 +23,7 @@
 
 
 C1, C2, C3 = -1640531535, 668265263, -2048144789
-CUT1, CUT2, CUT3 = 5, 9, 13
+CUT1, CUT2 = 6, 12
 C4 = wrap(-1028477387 << 8)
 
 
@@ -52,40 +52,63 @@
 
 def base_inverse(s, hook):
     n = 128
+    steps = n // 8
     rowid = lax.broadcasted_iota(jnp.int32, (8, 128), 0)
     lane = lax.broadcasted_iota(jnp.int32, (8, 128), 1)
-    top = [s[8 * i:8 * i + 8, :] for i in range(n // 8)]
-    aug = [(lane == rowid + 8 * i).astype(jnp.float32) for i in range(n // 8)]
+    top = [s[8 * i : 8 * i + 8, :] for i in range(steps)]
+    aug = [(lane == rowid + 8 * i).astype(jnp.float32) for i in range(steps)]
+
+    def across(x, k):
+        return jnp.broadcast_to(x[:, k : k + 1], (8, 128))
+
+    def down(x, j):
+        return jnp.broadcast_to(x[j : j + 1, :], (8, 128))
+
     done = []
-    for m in range(n // 8):
+    for m in range(steps):
         r, a = top[m], aug[m]
-        v = [jnp.broadcast_to(r[:, 8 * m + k:8 * m + k + 1], (8, 128)) for k in range(8)]
-        scale = jnp.zeros((8, 128), jnp.float32)
+        ahead = m + 1 < steps
+        v = [across(r, 8 * m + k) for k in range(8)]
+        if ahead:
+            nr, na = top[m + 1], aug[m + 1]
+            w = [across(nr, 8 * m + k) for k in range(8)]
         for j in range(8):
-            d = jnp.broadcast_to(v[j][j:j + 1, :], (8, 128))
-            scale = jnp.where(rowid == j, lax.rsqrt(d), scale)
-            if j < 7:
-                f = jnp.where(rowid > j, v[j] / d, 0.0)
-                for k in range(j + 1, 8):
-                    v[k] = v[k] - f * jnp.broadcast_to(v[k][j:j + 1, :], (8, 128))
-                r = r - f * jnp.broadcast_to(r[j:j + 1, :], (8, 128))
-                a = a - f * jnp.broadcast_to(a[j:j + 1, :], (8, 128))
-        r = r * scale
-        a = a * scale
+            root = lax.rsqrt(down(v[j], j))
+            f = jnp.where(rowid > j, v[j] * root, 0.0)
+            yr, ya = down(r, j) * root, down(a, j) * root
+            if ahead:
+                g = w[j] * root
+            for k in range(j + 1, 8):
+                q = down(v[k], j) * root
+                v[k] = v[k] - f * q
+                if ahead:
+                    w[k] = w[k] - g * q
+            r = jnp.where(rowid == j, yr, r - f * yr)
+            a = jnp.where(rowid == j, ya, a - f * ya)
+            if ahead:
+                nr = nr - g * yr
+                na = na - g * ya
         done.append(a)
-        hook(m)
-        if m < n // 8 - 1:
+        if ahead:
+            top[m + 1], aug[m + 1] = nr, na
+        if m + 2 < steps:
             ra, rb, rc = split3(r)
             aa, ab, ac = split3(a)
-            lo = 8 * (m + 1)
             left = jnp.concatenate([ra, ra, rb, ra, rb, rc], axis=0)
-            right = jnp.concatenate([jnp.concatenate([x, y], axis=1) for x, y in
-                                     ((ra, aa), (rb, ab), (ra, aa), (rc, ac), (rb, ab), (ra, aa))], axis=0)
-            u = lax.dot_general(left, right, TN, preferred_element_type=jnp.float32)
-            for i in range(m + 1, n // 8):
-                top[i] = top[i] - u[8 * i:8 * i + 8, :128]
-                aug[i] = aug[i] - u[8 * i:8 * i + 8, 128:]
+            right = jnp.concatenate(
+                [
+                    jnp.concatenate([x, y], axis=1)
+                    for x, y in ((ra, aa), (rb, ab), (ra, aa), (rc, ac), (rb, ab), (ra, aa))
+                ],
+                axis=0,
+            )
+            out = lax.dot_general(left, right, TN, preferred_element_type=jnp.float32)
+            for i in range(m + 2, steps):
+                top[i] = top[i] - out[8 * i : 8 * i + 8, :128]
+                aug[i] = aug[i] - out[8 * i : 8 * i + 8, 128:]
+        hook(m)
     return jnp.concatenate(done, axis=0)
+
 
 def factor_inverse(A, N, M, hook):
     for k in range(4):
@@ -256,17 +279,7 @@
     mine = fp.at[:, u, :, lanes(z)]
     panel_z = [go(mine, mine, pzs.at[d], pzr.at[d], to(ex=p)) for d, p in ex_peers]
 
-    blocks(CUT2, CUT3)
-    for one in panel_z:
-        one.wait_recv()
-
-    def panel_at(chip):
-        return fp.at[pl.ds(2 * c, 2), chip]
-
-    mine = panel_at(u)
-    panel_a = [go(mine, mine, pas.at[d], par.at[d], to(tp=p)) for d, p in chip_peers]
-
-    blocks(CUT3, TP)
+    blocks(CUT2, TP)
 
     @pl.when(t != 0)
     def _():
@@ -310,13 +323,14 @@
     pass_right(0, 0)
     pass_left(0, 0)
 
-    panel_over = []
-    for d in range(1, CHIPS):
-        panel_a[d - 1].wait_recv()
-        at = panel_at(lax.rem(u + CHIPS - d, CHIPS))
-        panel_over.append(go(at, at, pds.at[d], pdr.at[d], to(tp=other)))
-    for one in panel_over:
+    for one in panel_z:
         one.wait_recv()
+
+    def panel_at(chip):
+        return fp.at[pl.ds(2 * c, 2), chip]
+
+    mine = panel_at(u)
+    panel_a = [go(mine, mine, pas.at[d], par.at[d], to(tp=p)) for d, p in chip_peers]
 
     def along_blk():
         for j in range(1, BLK):
@@ -358,18 +372,30 @@
             at = row_at(lax.rem(u + CHIPS - d, CHIPS))
             rows_over.append(go(at, at, rds.at[d], rdr.at[d], to(tp=other)))
 
+    along_blk()
+    ring(1, (0,))
+
+    panel_over = []
+    for d in range(1, CHIPS):
+        panel_a[d - 1].wait_recv()
+        at = panel_at(lax.rem(u + CHIPS - d, CHIPS))
+        panel_over.append(go(at, at, pds.at[d], pdr.at[d], to(tp=other)))
+    for one in panel_over:
+        one.wait_recv()
+
     actions = {
-        (0, 12): (along_blk, rows_out),
-        (1, 2): (lambda: ring(1, (0,)),),
-        (1, 7): (lambda: ring(1, (1,)),),
-        (1, 11): (lambda: ring(1, (2,)),),
-        (1, 15): (lambda: ring(1, (3,)), lambda: ring(2, (0,))),
-        (2, 3): (lambda: ring(2, (1,)),),
-        (2, 7): (lambda: ring(2, (2,)),),
-        (2, 11): (lambda: ring(2, (3,)), lambda: ring(3, (0,))),
-        (2, 15): (lambda: ring(3, (1,)),),
-        (3, 3): (lambda: ring(3, (2,)),),
-        (3, 7): (lambda: ring(3, (3,)), rows_across),
+        (0, 3): (rows_out, lambda: ring(1, (1,))),
+        (0, 7): (lambda: ring(1, (2,)),),
+        (0, 11): (lambda: ring(1, (3,)),),
+        (1, 0): (lambda: ring(2, (0,)),),
+        (1, 3): (lambda: ring(2, (1,)),),
+        (1, 6): (lambda: ring(2, (2,)),),
+        (1, 9): (lambda: ring(2, (3,)),),
+        (1, 14): (lambda: ring(3, (0,)),),
+        (2, 2): (lambda: ring(3, (1,)),),
+        (2, 5): (lambda: ring(3, (2,)),),
+        (2, 8): (lambda: ring(3, (3,)),),
+        (2, 10): (rows_across,),
     }
 
     def hook(k, m):

time: 80.3 us -> 73.9 us (0.920)
  Pallas kernels: 75.2 us -> 68.2 us
    pallas_call x1, Pallas kernels: 75.2 us -> 68.2 us  [whole(): pl.pallas_call(whole_kernel, out_shape=(tile, tile), in_specs=[smem, smem...]
where the time goes in v3:
time: 73.9 us; the launch traced here: 72.8 us
  Pallas kernels  68.2 us (92%)
  local copies, waits for them, and re-layouts  2.72 us (4%)
  between operations  1.94 us (3%)
    pallas_call x1, Pallas kernels, whole(): pl.pallas_call(whole_kernel, out_shape=(tile, tile), in_specs=[smem, smem...  68.2 us
    unnamed x4, local copies, waits for them, and re-layouts  2.72 us

profile of v3, /device:TPU:1, one launch (start us, length us, event | category | flops | bytes accessed | tf_op | source)
XLA Modules:
  0.0 72.8 jit_solution(10952288364765572752)
XLA Ops:
  1.9 68.2 %whole.1 = (f32[256,512]{1,0:T(8,128)}, f32[256,512]{1,0:T(8,128)}) custom-call(s32[1]{0:T(128)S(6)} %copy.8.seed_ref, f32[1]{0:T(128)S(6)} %copy.9.ridge_ref, bf16[256,2048]{1,0:T(8,128)(2,1)} %grads_ref.1, s32[1,128]{1,0:T(1,128)} %bitcast.1), custom_call_target="tpu_custom_call" | custom-call | tf_op jit(solution)/shard_map/whole/pallas_call | solution.py:453
  70.1 0.0 copy-start
  70.1 1.9 %copy.10 = f32[256,512]{1,0:T(8,128)} copy(f32[256,512]{1,0:T(8,128)} %get-tuple-element.4) | data formatting | bytes 1048576
  72.0 0.0 copy-done
  72.0 0.8 %copy.11 = f32[256,512]{1,0:T(8,128)} copy(f32[256,512]{1,0:T(8,128)S(1)} %copy-done) | data formatting | bytes 1048576
Async XLA Ops:
  70.1 1.9 %copy-start = (f32[256,512]{1,0:T(8,128)S(1)}, f32[256,512]{1,0:T(8,128)}, u32[]{:S(2)}) copy-start(f32[256,512]{1,0:T(8,128)} %get-tuple-element.5) | copy-start | bytes 1572868

commit v4 on v3

--- a/solution.py
+++ b/solution.py
@@ -23,7 +23,7 @@
 
 
 C1, C2, C3 = -1640531535, 668265263, -2048144789
-CUT1, CUT2 = 6, 12
+CUT1, CUT2 = 6, 11
 C4 = wrap(-1028477387 << 8)
 
 
@@ -147,10 +147,10 @@
 
 
 def whole_kernel(
-    seed_ref, ridge_ref, grads_ref, sel_ref, pan, trail,
-    chosen_ref, cvec_ref, sign_ref, parts, fp, fr, fc, prx, rx, A, N, M, X,
+    seed_ref, ridge_ref, grads_hbm, sel_ref, pan, trail,
+    grads_ref, T, chosen_ref, cvec_ref, sign_ref, parts, fp, fr, fc, prx, rx, A, N, M, X,
     ps, pr, ms, mr, pys, pyr, mys, myr, rps, rpr, pzs, pzr,
-    rs_, rr_, ls_, lr_, ras, rar, rds, rdr, pas, par, pds, pdr, loc,
+    rs_, rr_, ls_, lr_, ras, rar, rds, rdr, pas, par, pds, pdr, loc, fetched,
 ):
     z, t, b = lax.axis_index("ex"), lax.axis_index("tp"), lax.axis_index("blk")
     u, c = t // 2, t % 2
@@ -199,17 +199,16 @@
     for _, p in ex_peers:
         greet(to(ex=p))
 
-    @pl.when(jnp.logical_not(alone))
-    def _():
-        greet(mate)
-
+    fetch = pltpu.make_async_copy(grads_hbm, grads_ref, fetched)
+    fetch.start()
     hot = (lax.broadcasted_iota(jnp.int32, (pool, SB), 0) == sel_ref[...]).astype(jnp.float32)
     hot = hot.astype(jnp.bfloat16)
+    cvec_ref[...] = (t * coords + lax.broadcasted_iota(jnp.int32, (8, coords), 1)) * jnp.int32(C1) + seed_ref[0]
+    fetch.wait()
     for s in range(coords // 256):
         chosen_ref[pl.ds(s * 256, 256), :] = lax.dot_general(
             grads_ref[:, s * 256 : (s + 1) * 256], hot, TN, preferred_element_type=jnp.float32
         ).astype(jnp.bfloat16)
-    cvec_ref[...] = (t * coords + lax.broadcasted_iota(jnp.int32, (8, coords), 1)) * jnp.int32(C1) + seed_ref[0]
 
     def product(block):
         first = block * PANEL + slot * SB
@@ -238,8 +237,7 @@
         parts[block] = out.astype(jnp.bfloat16)
 
     product(0)
-    greeted = len(tp_peers) + len(blk_peers) + len(ex_peers) + 1
-    pl.semaphore_wait(barrier, greeted - alone.astype(jnp.int32))
+    pl.semaphore_wait(barrier, len(tp_peers) + len(blk_peers) + len(ex_peers))
 
     panel_in = []
     for d, p in tp_peers:
@@ -285,6 +283,15 @@
     def _():
         product(t)
 
+    for one in panel_z:
+        one.wait_recv()
+
+    def panel_at(chip):
+        return fp.at[pl.ds(2 * c, 2), chip]
+
+    mine = panel_at(u)
+    panel_a = [go(mine, mine, pas.at[d], par.at[d], to(tp=p)) for d, p in chip_peers]
+
     for d in range(1, TP):
         share(d).wait_recv()
     total = parts[t].astype(jnp.float32)
@@ -297,14 +304,6 @@
     row_slot = fr.at[lanes(b // 2), lanes(z)]
     moved = copy(mine, row_slot, rps, rpr, mate)
 
-    @pl.when(alone)
-    def _():
-        pltpu.make_async_copy(mine, row_slot, loc).start()
-
-    @pl.when(jnp.logical_not(alone))
-    def _():
-        moved.start()
-
     right, left = to(ex=lax.rem(z + 1, EX)), to(ex=lax.rem(z + EX - 1, EX))
     rights, lefts = {}, {}
 
@@ -322,15 +321,6 @@
 
     pass_right(0, 0)
     pass_left(0, 0)
-
-    for one in panel_z:
-        one.wait_recv()
-
-    def panel_at(chip):
-        return fp.at[pl.ds(2 * c, 2), chip]
-
-    mine = panel_at(u)
-    panel_a = [go(mine, mine, pas.at[d], par.at[d], to(tp=p)) for d, p in chip_peers]
 
     def along_blk():
         for j in range(1, BLK):
@@ -383,19 +373,36 @@
     for one in panel_over:
         one.wait_recv()
 
+    @pl.when(alone)
+    def _():
+        pltpu.make_async_copy(piece(0, 0), row_slot, loc).start()
+
+    @pl.when(jnp.logical_not(alone))
+    def _():
+        moved.start()
+
+    def columns_here():
+        last = EX // 2 - 1
+        for j in range(BLK // 2):
+            rights[last, j].wait_recv()
+            lefts[last, BLK // 2 + j].wait_recv()
+        T[...] = gram(fp[...].reshape(PANEL, EXAMPLES), fc[...], 0, t * PANEL)
+
     actions = {
-        (0, 3): (rows_out, lambda: ring(1, (1,))),
+        (0, 3): (lambda: ring(1, (1,)),),
         (0, 7): (lambda: ring(1, (2,)),),
         (0, 11): (lambda: ring(1, (3,)),),
         (1, 0): (lambda: ring(2, (0,)),),
         (1, 3): (lambda: ring(2, (1,)),),
         (1, 6): (lambda: ring(2, (2,)),),
+        (1, 8): (rows_out,),
         (1, 9): (lambda: ring(2, (3,)),),
         (1, 14): (lambda: ring(3, (0,)),),
         (2, 2): (lambda: ring(3, (1,)),),
         (2, 5): (lambda: ring(3, (2,)),),
         (2, 8): (lambda: ring(3, (3,)),),
-        (2, 10): (rows_across,),
+        (3, 1): (columns_here,),
+        (3, 6): (rows_across,),
     }
 
     def hook(k, m):
@@ -415,10 +422,6 @@
     A[...] = gram(panel, panel, 0, 0)
     factor_inverse(A, N, M, hook)
 
-    last = EX // 2 - 1
-    for j in range(BLK // 2):
-        rights[last, j].wait_recv()
-        lefts[last, BLK // 2 + j].wait_recv()
     for one in rows_over:
         one.wait_recv()
     for one in pending:
@@ -427,7 +430,7 @@
         share(d).wait_send()
 
     panel = fp[...].reshape(PANEL, EXAMPLES)
-    X[...] = dot2(M[...], gram(panel, fc[...], 0, t * PANEL), NN)
+    X[...] = dot2(M[...], T[...], NN)
     first_tile = gram(fr[...], panel, g * 2 * SB, 0)
     own = gram(fr[...], fc[...], g * 2 * SB, t * PANEL)
     out = dot2(first_tile, M[...], NT)
@@ -445,7 +448,7 @@
     sems += [dma, dma, dma((EX,)), dma((EX,))]
     sems += [dma((EX // 2, BLK))] * 4
     sems += [dma((CHIPS,))] * 8
-    sems += [dma]
+    sems += [dma, dma]
     vmem = pl.BlockSpec(memory_space=pltpu.VMEM)
     smem = pl.BlockSpec(memory_space=pltpu.SMEM)
     tile = jax.ShapeDtypeStruct((2 * SB, PANEL), f32)
@@ -453,9 +456,11 @@
     return pl.pallas_call(
         whole_kernel,
         out_shape=(tile, tile),
-        in_specs=[smem, smem, vmem, vmem],
+        in_specs=[smem, smem, pl.BlockSpec(memory_space=pl.ANY), vmem],
         out_specs=(vmem, vmem),
         scratch_shapes=[
+            pltpu.VMEM(grads.shape, bf),
+            square,
             pltpu.VMEM((coords, SB), bf),
             pltpu.VMEM((8, coords), jnp.int32),
             pltpu.VMEM((SB, coords), bf),

time: 73.9 us -> 73.2 us (level)
  no operation moved by 1% of the time
where the time goes in v4:
time: 73.2 us; the launch traced here: 72.8 us
  Pallas kernels  68.1 us (93%)
  local copies, waits for them, and re-layouts  2.72 us (4%)
  between operations  1.94 us (3%)
    pallas_call x1, Pallas kernels, whole(): pl.pallas_call(whole_kernel, out_shape=(tile, tile), in_specs=[smem, smem...  68.1 us
    unnamed x4, local copies, waits for them, and re-layouts  2.72 us

profile of v4, /device:TPU:1, one launch (start us, length us, event | category | flops | bytes accessed | tf_op | source)
XLA Modules:
  0.0 72.8 jit_solution(3681073662100334671)
XLA Ops:
  1.9 68.1 %whole.1 = (f32[256,512]{1,0:T(8,128)}, f32[256,512]{1,0:T(8,128)}) custom-call(s32[1]{0:T(128)S(6)} %copy.8.seed_ref, f32[1]{0:T(128)S(6)} %copy.9.ridge_ref, bf16[256,2048]{1,0:T(8,128)(2,1)} %grads_hbm.1, s32[1,128]{1,0:T(1,128)} %bitcast.1), custom_call_target="tpu_custom_call" | custom-call | tf_op jit(solution)/shard_map/whole/pallas_call | solution.py:456
  70.0 0.0 copy-start
  70.1 1.9 %copy.10 = f32[256,512]{1,0:T(8,128)} copy(f32[256,512]{1,0:T(8,128)} %get-tuple-element.4) | data formatting | bytes 1048576
  72.0 0.0 copy-done
  72.0 0.8 %copy.11 = f32[256,512]{1,0:T(8,128)} copy(f32[256,512]{1,0:T(8,128)S(1)} %copy-done) | data formatting | bytes 1048576
Async XLA Ops:
  70.0 1.9 %copy-start = (f32[256,512]{1,0:T(8,128)S(1)}, f32[256,512]{1,0:T(8,128)}, u32[]{:S(2)}) copy-start(f32[256,512]{1,0:T(8,128)} %get-tuple-element.5) | copy-start | bytes 1572868

commit v5 on v4

--- a/solution.py
+++ b/solution.py
@@ -286,11 +286,15 @@
     for one in panel_z:
         one.wait_recv()
 
-    def panel_at(chip):
-        return fp.at[pl.ds(2 * c, 2), chip]
-
-    mine = panel_at(u)
-    panel_a = [go(mine, mine, pas.at[d], par.at[d], to(tp=p)) for d, p in chip_peers]
+    def panel_at(chip, half):
+        return fp.at[2 * c + half, chip]
+
+    panel_a = []
+    for half in range(2):
+        mine = panel_at(u, half)
+        for d, p in chip_peers:
+            k = half * CHIPS + d
+            panel_a.append(go(mine, mine, pas.at[k], par.at[k], to(tp=p)))
 
     for d in range(1, TP):
         share(d).wait_recv()
@@ -366,12 +370,20 @@
     ring(1, (0,))
 
     panel_over = []
-    for d in range(1, CHIPS):
-        panel_a[d - 1].wait_recv()
-        at = panel_at(lax.rem(u + CHIPS - d, CHIPS))
-        panel_over.append(go(at, at, pds.at[d], pdr.at[d], to(tp=other)))
-    for one in panel_over:
-        one.wait_recv()
+
+    def panel_across(half):
+        for d in range(1, CHIPS):
+            panel_a[half * (CHIPS - 1) + d - 1].wait_recv()
+            at = panel_at(lax.rem(u + CHIPS - d, CHIPS), half)
+            k = half * CHIPS + d
+            panel_over.append(go(at, at, pds.at[k], pdr.at[k], to(tp=other)))
+
+    def panel_done(half):
+        for one in panel_over[half * (CHIPS - 1) :]:
+            one.wait_recv()
+
+    panel_across(0)
+    panel_done(0)
 
     @pl.when(alone)
     def _():
@@ -388,10 +400,17 @@
             lefts[last, BLK // 2 + j].wait_recv()
         T[...] = gram(fp[...].reshape(PANEL, EXAMPLES), fc[...], 0, t * PANEL)
 
+    def panel_here():
+        panel_done(1)
+        panel = fp[...].reshape(PANEL, EXAMPLES)
+        A[...] = gram(panel, panel, 0, 0)
+
     actions = {
         (0, 3): (lambda: ring(1, (1,)),),
         (0, 7): (lambda: ring(1, (2,)),),
         (0, 11): (lambda: ring(1, (3,)),),
+        (0, 12): (lambda: panel_across(1),),
+        (0, 15): (panel_here,),
         (1, 0): (lambda: ring(2, (0,)),),
         (1, 3): (lambda: ring(2, (1,)),),
         (1, 6): (lambda: ring(2, (2,)),),
@@ -418,8 +437,8 @@
         rows_, cols_ = (lax.broadcasted_iota(jnp.int32, out.shape, k) for k in range(2))
         return out + jnp.where(rows_ + r0 == cols_ + c0, rv, 0.0)
 
-    panel = fp[...].reshape(PANEL, EXAMPLES)
-    A[...] = gram(panel, panel, 0, 0)
+    corner = fp[0].reshape(SB, EXAMPLES)
+    A[:SB, :SB] = gram(corner, corner, 0, 0)
     factor_inverse(A, N, M, hook)
 
     for one in rows_over:
@@ -447,7 +466,7 @@
         sems += [dma((n,)), dma((n,))]
     sems += [dma, dma, dma((EX,)), dma((EX,))]
     sems += [dma((EX // 2, BLK))] * 4
-    sems += [dma((CHIPS,))] * 8
+    sems += [dma((CHIPS,))] * 4 + [dma((2 * CHIPS,))] * 4
     sems += [dma, dma]
     vmem = pl.BlockSpec(memory_space=pltpu.VMEM)
     smem = pl.BlockSpec(memory_space=pltpu.SMEM)

time: 73.2 us -> 75.8 us (1.036)
  the two profiles are of different devices: /device:TPU:1 before, /device:TPU:9 now
where the time goes in v5:
time: 75.8 us; the launch traced here: 75.6 us
  Pallas kernels  70.9 us (94%)
  local copies, waits for them, and re-layouts  2.72 us (4%)
  between operations  1.94 us (3%)
    pallas_call x1, Pallas kernels, whole(): pl.pallas_call(whole_kernel, out_shape=(tile, tile), in_specs=[smem, smem...  70.9 us
    unnamed x4, local copies, waits for them, and re-layouts  2.72 us

profile of v5, /device:TPU:9, one launch (start us, length us, event | category | flops | bytes accessed | tf_op | source)
XLA Modules:
  0.0 75.6 jit_solution(8109341961993431769)
XLA Ops:
  1.9 70.9 %whole.1 = (f32[256,512]{1,0:T(8,128)}, f32[256,512]{1,0:T(8,128)}) custom-call(s32[1]{0:T(128)S(6)} %copy.8.seed_ref, f32[1]{0:T(128)S(6)} %copy.9.ridge_ref, bf16[256,2048]{1,0:T(8,128)(2,1)} %grads_hbm.1, s32[1,128]{1,0:T(1,128)} %bitcast.1), custom_call_target="tpu_custom_call" | custom-call | tf_op jit(solution)/shard_map/whole/pallas_call | solution.py:475
  72.8 0.0 copy-start
  72.8 1.9 %copy.10 = f32[256,512]{1,0:T(8,128)} copy(f32[256,512]{1,0:T(8,128)} %get-tuple-element.4) | data formatting | bytes 1048576
  74.8 0.0 copy-done
  74.8 0.8 %copy.11 = f32[256,512]{1,0:T(8,128)} copy(f32[256,512]{1,0:T(8,128)S(1)} %copy-done) | data formatting | bytes 1048576
Async XLA Ops:
  72.8 1.9 %copy-start = (f32[256,512]{1,0:T(8,128)S(1)}, f32[256,512]{1,0:T(8,128)}, u32[]{:S(2)}) copy-start(f32[256,512]{1,0:T(8,128)} %get-tuple-element.5) | copy-start | bytes 1572868

commit v6 on v4

--- a/solution.py
+++ b/solution.py
@@ -362,14 +362,13 @@
             at = row_at(lax.rem(u + CHIPS - d, CHIPS))
             rows_over.append(go(at, at, rds.at[d], rdr.at[d], to(tp=other)))
 
-    along_blk()
-    ring(1, (0,))
-
     panel_over = []
     for d in range(1, CHIPS):
         panel_a[d - 1].wait_recv()
         at = panel_at(lax.rem(u + CHIPS - d, CHIPS))
         panel_over.append(go(at, at, pds.at[d], pdr.at[d], to(tp=other)))
+    along_blk()
+    ring(1, (0,))
     for one in panel_over:
         one.wait_recv()
 

time: 73.2 us -> 74 us (1.011)
  the two profiles are of different devices: /device:TPU:1 before, /device:TPU:8 now
where the time goes in v6:
time: 74 us; the launch traced here: 73.8 us
  Pallas kernels  69.1 us (93%)
  local copies, waits for them, and re-layouts  2.72 us (4%)
  between operations  1.94 us (3%)
    pallas_call x1, Pallas kernels, whole(): pl.pallas_call(whole_kernel, out_shape=(tile, tile), in_specs=[smem, smem...  69.1 us
    unnamed x4, local copies, waits for them, and re-layouts  2.72 us

profile of v6, /device:TPU:8, one launch (start us, length us, event | category | flops | bytes accessed | tf_op | source)
XLA Modules:
  0.0 73.8 jit_solution(13218332635745869119)
XLA Ops:
  1.9 69.1 %whole.1 = (f32[256,512]{1,0:T(8,128)}, f32[256,512]{1,0:T(8,128)}) custom-call(s32[1]{0:T(128)S(6)} %copy.8.seed_ref, f32[1]{0:T(128)S(6)} %copy.9.ridge_ref, bf16[256,2048]{1,0:T(8,128)(2,1)} %grads_hbm.1, s32[1,128]{1,0:T(1,128)} %bitcast.1), custom_call_target="tpu_custom_call" | custom-call | tf_op jit(solution)/shard_map/whole/pallas_call | solution.py:455
  71.1 0.0 copy-start
  71.1 1.9 %copy.10 = f32[256,512]{1,0:T(8,128)} copy(f32[256,512]{1,0:T(8,128)} %get-tuple-element.4) | data formatting | bytes 1048576
  73.0 0.0 copy-done
  73.0 0.8 %copy.11 = f32[256,512]{1,0:T(8,128)} copy(f32[256,512]{1,0:T(8,128)S(1)} %copy-done) | data formatting | bytes 1048576
Async XLA Ops:
  71.1 1.9 %copy-start = (f32[256,512]{1,0:T(8,128)S(1)}, f32[256,512]{1,0:T(8,128)}, u32[]{:S(2)}) copy-start(f32[256,512]{1,0:T(8,128)} %get-tuple-element.5) | copy-start | bytes 1572868
